TPU v7x, 256 devices: a whole 4x4x8 slice. The times are simulated.
256 devices in a mesh: frames: 16 (over y, x), pix: 16 (over z, core).
Axes of the slice: x: 4, y: 4, z: 8, core: 2. Of those that a mesh axis runs over, the one named last changes fastest.
Arguments:
- photon_counts: int32 [16384, 32768], P('frames', 'pix'), may hold values from 1 to 53, as said below
- flat_field: float32 [32768], P('pix'), may hold values from 0.5 to 2
- owner_counts: int32 [16], replicated, may hold values from 512 to 2048, as said below
Outputs:
- diagonal_tiles: float32 [16384, 1024], P(('frames', 'pix'))
- offdiag_tiles: float32 [16384, 1024], P(('frames', 'pix'))
Inputs may be any that keep to these rules, and one draw needn't show every extreme that they name: owner_counts[i] is how many of owner i's 2048 slots, the first ones, hold cycle pixels; some owner holds all 2048. `photon_counts`: whole photon counts of each slot in each frame.
All inputs are finite; a program needn't handle non-finite values.
Results may differ from a plain program's by a relative error of at most 0.0003.
Values may be sent and summed in bfloat16 or wider, within the bound.
No kernel may reach another device: no remote copies, remote signals or barrier semaphores. Data moves between devices by JAX's collectives and lax.ppermute only.
A program may use at most 64 MiB of HBM per device.

v0:
```python
import jax
import jax.numpy as jnp
from jax import lax
from jax.sharding import PartitionSpec as P


def shifted(value, axis, steps):
    count = lax.axis_size(axis)
    leading, last = (max(0, -steps), min(count, count - steps))
    return lax.ppermute(value, axis, [(source, source + steps) for source in range(leading, last)])


def gram(left, right):
    return lax.dot_general(
        left, right, (((1,), (1,)), ((), ())), preferred_element_type=jnp.float32
    )


def on_device(photon_counts, flat_field, owner_counts):
    owner_index = lax.axis_index("pix")
    slot_count = flat_field.shape[0]
    limit = owner_counts[owner_index]
    valid = (jnp.arange(slot_count, dtype=jnp.int32) < limit).astype(jnp.float32)
    weights = flat_field * valid
    pixel_total = jnp.sum(owner_counts).astype(jnp.float32)
    corrected = photon_counts.astype(jnp.float32) * weights[None, :]
    frame_sums = lax.psum(jnp.sum(corrected, axis=1), "pix")
    frame_mean = frame_sums / pixel_total
    scaled = (corrected / frame_mean[:, None]).astype(jnp.bfloat16)
    earlier = shifted(scaled, "frames", 1)
    diagonal_part = gram(scaled, scaled)
    offdiag_part = gram(scaled, earlier)
    diagonal_rows, offdiag_rows = (
        lax.psum_scatter(diagonal_part, "pix", scatter_dimension=0, tiled=True),
        lax.psum_scatter(offdiag_part, "pix", scatter_dimension=0, tiled=True),
    )
    return (diagonal_rows / pixel_total, offdiag_rows / pixel_total)


def solution(mesh):
    placed = (P("frames", "pix"), P("pix"), P())
    return jax.shard_map(
        on_device,
        mesh=mesh,
        in_specs=placed,
        out_specs=(P(("frames", "pix"), None), P(("frames", "pix"), None)),
        check_vma=False,
    )
```

profile of v0, /device:TPU:4, one launch (start us, length us, event | category | flops | bytes accessed | tf_op | source)
XLA Modules:
  0.0 229.9 jit_solution(11352595881727451091)
XLA Ops:
  7.2 0.0 reduce-scatter.3.cloned.1.call-start
  7.2 1.3 reduce_sum.19
  8.5 1.2 dynamic_slice.3
  9.7 1.3 fusion.1
  11.1 4.3 %fusion = f32[1024]{0:T(1024)S(1)} fusion(s32[1024,2048]{1,0:T(8,128)} %param.3, f32[2048]{0:T(1024)S(1)} %fusion.1), kind=kLoop, calls=%fused_computation.2 | loop fusion | flops 6290432 | bytes 8400896 | tf_op jit(solution)/shard_map/reduce_sum | solution.py:27
  15.4 28.8 %psum.7 = f32[1024]{0:T(1024)S(1)} all-reduce(f32[1024]{0:T(1024)S(1)} %fusion), channel_id=1, replica_groups=mesh['frames'=16,'pix'=16] {'pix'}, use_global_device_ids=true, to_apply=%region_1.0 | all-reduce | flops 1024 | bytes 8192 | tf_op jit(solution)/shard_map/psum | solution.py:27
  44.9 4.3 %divide_convert_fusion = bf16[1024,2048]{1,0:T(8,128)(2,1)S(1)} fusion(s32[1024,2048]{1,0:T(8,128)} %param.3, f32[1024]{0:T(1024)S(1)} %broadcast_divide_fusion.2, f32[2048]{0:T(1024)S(1)} %fusion.1), kind=kLoop, calls=%fused_computation | loop fusion | flops 8388608 | bytes 12595200 | tf_op jit(solution)/shard_map/convert_element_type | solution.py:29
  49.2 0.0 copy-start
  49.2 2.0 copy-done
  51.2 6.1 %fusion.2 = f32[1024,1024]{1,0:T(8,128)} fusion(bf16[1024,2048]{1,0:T(8,128)(2,1)S(1)} %divide_convert_fusion), kind=kOutput, calls=%fused_computation.8 | convolution fusion | flops 4294967296 | bytes 8388608 | tf_op jit(solution)/shard_map/dot_general | solution.py:14
  57.3 0.0 reduce-scatter.3.cloned.1.call-update
  57.3 0.0 reduce-scatter.5.cloned.1.call-start
  57.3 3.1 %collective-permute-start = (bf16[1024,2048]{1,0:T(8,128)(2,1)}, bf16[1024,2048]{1,0:T(8,128)(2,1)S(1)}, u32[]{:S(2)}, u32[]{:S(2)}) collective-permute-start(bf16[1024,2048]{1,0:T(8,128)(2,1)} %copy-done), channel_id=1, source_target_pairs={{0,16},{16,32},{32,48},{48,64},{64,80},{80,96},{96,112},{112,128},... | collective-permute-start | bytes 12582920 | tf_op jit(solution)/shard_map/ppermute | solution.py:10
  60.4 89.1 %collective-permute-done = bf16[1024,2048]{1,0:T(8,128)(2,1)S(1)} collective-permute-done((bf16[1024,2048]{1,0:T(8,128)(2,1)}, bf16[1024,2048]{1,0:T(8,128)(2,1)S(1)}, u32[]{:S(2)}, u32[]{:S(2)}) %collective-permute-start) | collective-permute-done | bytes 4194336 | tf_op jit(solution)/shard_map/ppermute | solution.py:10
  149.5 8.4 %fusion.3 = f32[1024,1024]{1,0:T(8,128)} fusion(bf16[1024,2048]{1,0:T(8,128)(2,1)} %copy-done, bf16[1024,2048]{1,0:T(8,128)(2,1)S(1)} %collective-permute-done), kind=kOutput, calls=%fused_computation.9 | convolution fusion | flops 4294967296 | bytes 12582912 | tf_op jit(solution)/shard_map/dot_general | solution.py:14
  157.9 0.0 reduce-scatter.5.cloned.1.call-update
  157.9 0.0 reduce-scatter.3.cloned.1.call-done
  157.9 1.7 broadcast_divide_fusion.1
  159.6 61.8 %reduce-scatter.5.cloned.1.call-done = f32[64,1024]{1,0:T(8,128)} async-done(((f32[1024,1024]{1,0:T(8,128)}), f32[64,1024]{1,0:T(8,128)}) %reduce-scatter.5.cloned.1.call-update) | async-done | bytes 262160 | tf_op jit(solution)/shard_map/reduce_scatter | solution.py:35
  221.4 1.7 broadcast_divide_fusion
  (1 shorter events, 0.0 us)
Async XLA Ops:
  7.2 150.8 %reduce-scatter.3.cloned.1.call-start = ((), (), s32[]{:S(2)}) async-start(), calls=%async_computation.2 | async-start | bytes 4456448 | tf_op jit(solution)/shard_map/reduce_scatter | solution.py:34
  49.2 2.0 copy-start
  57.3 164.1 %reduce-scatter.5.cloned.1.call-start = ((), (), s32[]{:S(2)}) async-start(), calls=%async_computation.3 | async-start | bytes 4456448 | tf_op jit(solution)/shard_map/reduce_scatter | solution.py:35
  57.3 92.2 %collective-permute-start = (bf16[1024,2048]{1,0:T(8,128)(2,1)}, bf16[1024,2048]{1,0:T(8,128)(2,1)S(1)}, u32[]{:S(2)}, u32[]{:S(2)}) collective-permute-start(bf16[1024,2048]{1,0:T(8,128)(2,1)} %copy-done), channel_id=1, source_target_pairs={{0,16},{16,32},{32,48},{48,64},{64,80},{80,96},{96,112},{112,128},... | collective-permute-start | bytes 12582920 | tf_op jit(solution)/shard_map/ppermute | solution.py:10
Sparse Core Ops, SparseCore 0:
  57.4 60.8 reduce-scatter.2
  158.0 63.3 reduce-scatter.4
where the time goes:
time: 230 us
  waiting for transfers between devices  151 us (66%)
  blocking collectives  28.8 us (13%)
  between operations  14.7 us (6%)
  other arithmetic  14.6 us (6%)
  matrix products  14.4 us (6%)
  local copies, waits for them, and re-layouts  3.2 us (1%)
  starting transfers between devices  3.19 us (1%)
    ppermute x1, waiting for transfers between devices, shifted(): lax.ppermute(value, axis, [(source, source + steps) for source in range(l...  89.1 us
    reduce_scatter x1, waiting for transfers between devices, on_device(): lax.psum_scatter(offdiag_part, 'pix', scatter_dimension=0, tiled=True)  61.8 us
    psum x1, blocking collectives, on_device(): frame_sums = lax.psum(jnp.sum(corrected, axis=1), 'pix')  28.8 us
    dot_general x2, matrix products, gram(): lax.dot_general(left, right, (((1,), (1,)), ((), ())), preferred_element_...  14.4 us
  transfers between devices with their start and end apart: 3, of which 2 were waited for; matrix products, arithmetic and copies ran while one was open for 4% of the time, Pallas kernels for 0%

commit v1 on v0

--- a/solution.py
+++ b/solution.py
@@ -24,7 +24,7 @@
     weights = flat_field * valid
     pixel_total = jnp.sum(owner_counts).astype(jnp.float32)
     corrected = photon_counts.astype(jnp.float32) * weights[None, :]
-    frame_sums = lax.psum(jnp.sum(corrected, axis=1), "pix")
+    frame_sums = jnp.sum(lax.all_gather(jnp.sum(corrected, axis=1), "pix"), axis=0)
     frame_mean = frame_sums / pixel_total
     scaled = (corrected / frame_mean[:, None]).astype(jnp.bfloat16)
     earlier = shifted(scaled, "frames", 1)

time: 230 us -> 223 us (0.970)
  blocking collectives: 28.8 us -> 20.1 us
    psum x1 -> x0, blocking collectives: 28.8 us -> none  [on_device(): frame_sums = lax.psum(jnp.sum(corrected, axis=1), 'pix')]
    all_gather x0 -> x1, blocking collectives: none -> 20.1 us  [on_device(): lax.all_gather(jnp.sum(corrected, axis=1), 'pix')]
    ppermute x1, waiting for transfers between devices: 89.1 us -> 91.8 us  [shifted(): lax.ppermute(value, axis, [(source, source + steps) for source in range(l...]
  transfers between devices with their start and end apart: 3 -> 3, of which waited for: 2 -> 2; matrix products, arithmetic and copies ran while one was open for 4% -> 5% of each run, Pallas kernels for 0% -> 0%
where the time goes in v1:
time: 223 us; the launch traced here: 222 us
  waiting for transfers between devices  152 us (68%)
  blocking collectives  20.1 us (9%)
  between operations  14.7 us (7%)
  other arithmetic  14.6 us (7%)
  matrix products  14.4 us (6%)
  local copies, waits for them, and re-layouts  3.22 us (1%)
  starting transfers between devices  3.18 us (1%)
    ppermute x1, waiting for transfers between devices, shifted(): lax.ppermute(value, axis, [(source, source + steps) for source in range(l...  91.8 us
    reduce_scatter x1, waiting for transfers between devices, on_device(): lax.psum_scatter(offdiag_part, 'pix', scatter_dimension=0, tiled=True)  59.8 us
    all_gather x1, blocking collectives, on_device(): lax.all_gather(jnp.sum(corrected, axis=1), 'pix')  20.1 us
    dot_general x2, matrix products, gram(): lax.dot_general(left, right, (((1,), (1,)), ((), ())), preferred_element_...  14.4 us
  transfers between devices with their start and end apart: 3, of which 2 were waited for; matrix products, arithmetic and copies ran while one was open for 5% of the time, Pallas kernels for 0%

profile of v1, /device:TPU:4, one launch (start us, length us, event | category | flops | bytes accessed | tf_op | source)
XLA Modules:
  0.0 222.0 jit_solution(1555571836613258133)
XLA Ops:
  7.2 0.0 reduce-scatter.3.cloned.1.call-start
  7.2 1.3 reduce_sum.29
  8.5 1.2 dynamic_slice.3
  9.7 1.3 fusion.1
  11.1 4.3 %fusion = f32[1024]{0:T(1024)S(1)} fusion(s32[1024,2048]{1,0:T(8,128)} %param.3, f32[2048]{0:T(1024)S(1)} %fusion.1), kind=kLoop, calls=%fused_computation.2 | loop fusion | flops 6290432 | bytes 8400896 | tf_op jit(solution)/shard_map/reduce_sum | solution.py:27
  15.4 20.1 %all-gather = f32[16384]{0:T(1024)S(1)} all-gather(f32[1024]{0:T(1024)S(1)} %fusion), channel_id=2, replica_groups=mesh['frames'=16,'pix'=16] {'pix'}, dimensions={0}, use_global_device_ids=true | all-gather | bytes 69632 | tf_op jit(solution)/shard_map/all_gather | solution.py:27
  36.2 4.3 %divide_convert_fusion = bf16[1024,2048]{1,0:T(8,128)(2,1)S(1)} fusion(s32[1024,2048]{1,0:T(8,128)} %param.3, f32[1024]{0:T(1024)S(1)} %broadcast_divide_fusion.2, f32[2048]{0:T(1024)S(1)} %fusion.1), kind=kLoop, calls=%fused_computation | loop fusion | flops 8388608 | bytes 12595200 | tf_op jit(solution)/shard_map/convert_element_type | solution.py:29
  40.5 0.0 copy-start
  40.6 2.0 copy-done
  42.5 6.1 %fusion.2 = f32[1024,1024]{1,0:T(8,128)} fusion(bf16[1024,2048]{1,0:T(8,128)(2,1)S(1)} %divide_convert_fusion), kind=kOutput, calls=%fused_computation.8 | convolution fusion | flops 4294967296 | bytes 8388608 | tf_op jit(solution)/shard_map/dot_general | solution.py:14
  48.6 0.0 reduce-scatter.3.cloned.1.call-update
  48.6 0.0 reduce-scatter.5.cloned.1.call-start
  48.7 3.1 %collective-permute-start = (bf16[1024,2048]{1,0:T(8,128)(2,1)}, bf16[1024,2048]{1,0:T(8,128)(2,1)S(1)}, u32[]{:S(2)}, u32[]{:S(2)}) collective-permute-start(bf16[1024,2048]{1,0:T(8,128)(2,1)} %copy-done), channel_id=1, source_target_pairs={{0,16},{16,32},{32,48},{48,64},{64,80},{80,96},{96,112},{112,128},... | collective-permute-start | bytes 12582920 | tf_op jit(solution)/shard_map/ppermute | solution.py:10
  51.8 91.8 %collective-permute-done = bf16[1024,2048]{1,0:T(8,128)(2,1)S(1)} collective-permute-done((bf16[1024,2048]{1,0:T(8,128)(2,1)}, bf16[1024,2048]{1,0:T(8,128)(2,1)S(1)}, u32[]{:S(2)}, u32[]{:S(2)}) %collective-permute-start) | collective-permute-done | bytes 4194336 | tf_op jit(solution)/shard_map/ppermute | solution.py:10
  143.6 8.4 %fusion.3 = f32[1024,1024]{1,0:T(8,128)} fusion(bf16[1024,2048]{1,0:T(8,128)(2,1)} %copy-done, bf16[1024,2048]{1,0:T(8,128)(2,1)S(1)} %collective-permute-done), kind=kOutput, calls=%fused_computation.9 | convolution fusion | flops 4294967296 | bytes 12582912 | tf_op jit(solution)/shard_map/dot_general | solution.py:14
  152.0 0.0 reduce-scatter.5.cloned.1.call-update
  152.0 0.0 reduce-scatter.3.cloned.1.call-done
  152.0 1.7 broadcast_divide_fusion.1
  153.7 59.8 %reduce-scatter.5.cloned.1.call-done = f32[64,1024]{1,0:T(8,128)} async-done(((f32[1024,1024]{1,0:T(8,128)}), f32[64,1024]{1,0:T(8,128)}) %reduce-scatter.5.cloned.1.call-update) | async-done | bytes 262160 | tf_op jit(solution)/shard_map/reduce_scatter | solution.py:35
  213.5 1.7 broadcast_divide_fusion
  (3 shorter events, 0.0 us)
Async XLA Ops:
  7.2 144.9 %reduce-scatter.3.cloned.1.call-start = ((), (), s32[]{:S(2)}) async-start(), calls=%async_computation.2 | async-start | bytes 4456448 | tf_op jit(solution)/shard_map/reduce_scatter | solution.py:34
  40.5 2.0 copy-start
  48.6 164.8 %reduce-scatter.5.cloned.1.call-start = ((), (), s32[]{:S(2)}) async-start(), calls=%async_computation.3 | async-start | bytes 4456448 | tf_op jit(solution)/shard_map/reduce_scatter | solution.py:35
  48.7 94.9 %collective-permute-start = (bf16[1024,2048]{1,0:T(8,128)(2,1)}, bf16[1024,2048]{1,0:T(8,128)(2,1)S(1)}, u32[]{:S(2)}, u32[]{:S(2)}) collective-permute-start(bf16[1024,2048]{1,0:T(8,128)(2,1)} %copy-done), channel_id=1, source_target_pairs={{0,16},{16,32},{32,48},{48,64},{64,80},{80,96},{96,112},{112,128},... | collective-permute-start | bytes 12582920 | tf_op jit(solution)/shard_map/ppermute | solution.py:10
Sparse Core Ops, SparseCore 0:
  48.8 61.3 reduce-scatter.2
  152.1 61.3 reduce-scatter.4
